TPU v7x, 256 devices: a whole 4x4x8 slice. The times are simulated.
256 devices in a mesh: ctx: 32 (over x, y, core), ch: 8 (over z).
Axes of the slice: x: 4, y: 4, z: 8, core: 2. Of those that a mesh axis runs over, the one named last changes fastest.
Arguments:
- gate_input: bfloat16 [8192, 16384], P('ch', 'ctx'), may hold values from -90 to 90
- key_input: bfloat16 [8192, 16384], P('ch', 'ctx'), may hold values from -6 to 6
- value_input: bfloat16 [8192, 16384], P('ch', 'ctx'), may hold values from -6 to 6
- short_filter: float32 [3, 3, 8192], P(None, None, 'ch'), may hold values from -3.5 to 3.5
- mr_filter: float32 [512, 128], P('ch'), may hold values from -0.5 to 0.5
- mr_skip: float32 [8192], P('ch'), may hold values from -3 to 3
- norm_gain: float32 [8192], P('ch'), may hold values from 0.5 to 1.5
- doc_lengths: int32 [64], replicated, may hold values from 1 to 2048, 16384 in all
Outputs:
- relaid: bfloat16 [8192, 16384], P(('ch', 'ctx'))
Inputs may be any that keep to these rules, and one draw needn't show every extreme that they name: `doc_lengths`: the 64 lengths sum to 16384, and one of them is exactly 2048.
All inputs are finite; a program needn't handle non-finite values.
Results may differ from a plain program's by a relative error of at most 0.0095.
Values may be sent and summed in bfloat16 or wider, within the bound.
No kernel may reach another device: no remote copies, remote signals or barrier semaphores. Data moves between devices by JAX's collectives and lax.ppermute only.
A program may use at most 128 MiB of HBM per device.

v0:
```python
import math
import jax
import jax.numpy as jnp
from jax import lax
from jax.sharding import PartitionSpec as P

D = 8192
GROUP = 16
SHORT = 3
MR = 128
NORM_EPS = 1e-06


def doc_starts(doc_lengths, positions):
    doc_ends = jnp.cumsum(doc_lengths)
    doc_firsts = doc_ends - doc_lengths
    before_row = doc_firsts[:, None] <= positions[None, :]
    return jnp.max(jnp.where(before_row, doc_firsts[:, None], 0), axis=0)


def short_conv(raw_rows, prior_rows, tap_rows, positions, starts):
    row_count = raw_rows.shape[1]
    extended = jnp.concatenate([prior_rows, raw_rows], axis=1).astype(jnp.float32)
    running = jnp.zeros(raw_rows.shape, jnp.float32)
    for tap_lag in range(SHORT):
        lagged = lax.slice_in_dim(
            extended, SHORT - 1 - tap_lag, SHORT - 1 - tap_lag + row_count, axis=1
        )
        in_document = positions - tap_lag >= starts
        running = running + jnp.where(
            in_document[None, :], tap_rows[tap_lag][:, None] * lagged, 0.0
        )
    return running


def features(raw_list, prior_list, short_taps, positions, starts):
    gate_conv = short_conv(raw_list[0], prior_list[0], short_taps[0], positions, starts)
    key_conv = short_conv(raw_list[1], prior_list[1], short_taps[1], positions, starts)
    value_conv = short_conv(raw_list[2], prior_list[2], short_taps[2], positions, starts)
    return (gate_conv, (key_conv * value_conv).astype(jnp.bfloat16))


def toeplitz(taps_bf):
    groups = taps_bf.shape[0]
    padded = jnp.concatenate(
        [jnp.zeros((groups, MR), jnp.bfloat16), taps_bf, jnp.zeros((groups, MR + 1), jnp.bfloat16)],
        axis=1,
    )
    repeated = jnp.tile(padded, (1, 2 * MR))[:, : 2 * MR * 3 * MR].reshape(groups, 2 * MR, 3 * MR)
    return repeated[:, :, 2 * MR :]


def long_conv(values, prior_rows, taps_bf, starts):
    channels, row_count = values.shape
    groups = taps_bf.shape[0]
    members = channels // groups
    tile_count = row_count // MR
    blocked = jnp.concatenate([prior_rows, values], axis=1).reshape(channels, tile_count + 1, MR)
    windows = jnp.concatenate([blocked[:, :-1], blocked[:, 1:]], axis=2).reshape(
        groups, members, tile_count, 2 * MR
    )
    matrices = toeplitz(taps_bf)
    per_step = math.gcd(tile_count, max(1, 64 // groups))
    tile_starts = starts.reshape(tile_count, MR)
    source_offsets = jnp.arange(2 * MR, dtype=jnp.int32) - MR
    step_offsets = jnp.arange(per_step, dtype=jnp.int32) * MR
    zero_bf = jnp.zeros((), jnp.bfloat16)

    def advance(step_index, result):
        block_begin = step_index * per_step
        window_part = lax.dynamic_slice_in_dim(windows, block_begin, per_step, axis=2)
        row_starts = lax.dynamic_slice_in_dim(tile_starts, block_begin, per_step, axis=0)
        tile_first = block_begin * MR + step_offsets
        sources = tile_first[:, None] + source_offsets[None, :]
        allowed = sources[:, :, None] >= row_starts[:, None, :]
        masked = jnp.where(allowed[:, None], matrices[None], zero_bf)
        product = jnp.einsum(
            "gcns,ngst->gcnt", window_part, masked, preferred_element_type=jnp.float32
        )
        return lax.dynamic_update_slice_in_dim(result, product, block_begin, axis=2)

    result = lax.fori_loop(
        0,
        tile_count // per_step,
        advance,
        jnp.zeros((groups, members, tile_count, MR), jnp.float32),
    )
    return result.reshape(channels, row_count)


def row_total(partial_value):
    return lax.psum(partial_value, "ch")


def local(
    gate_input, key_input, value_input, short_filter, mr_filter, mr_skip, norm_gain, doc_lengths
):
    ctx_place = lax.axis_index("ctx")
    stacked = jnp.stack([gate_input, key_input, value_input])
    received = lax.all_to_all(stacked, "ctx", split_axis=1, concat_axis=2, tiled=True)
    narrow = received.shape[1]
    all_rows = received.shape[2]
    chan_offset = ctx_place * narrow
    positions = jnp.arange(all_rows, dtype=jnp.int32)
    starts = doc_starts(doc_lengths, positions)
    short_taps = lax.dynamic_slice_in_dim(short_filter, chan_offset, narrow, axis=2)
    zero_prior = jnp.zeros((narrow, SHORT - 1), jnp.bfloat16)
    gate_conv, product_rows = features(
        [received[0], received[1], received[2]],
        [zero_prior, zero_prior, zero_prior],
        short_taps,
        positions,
        starts,
    )
    group_rows = lax.dynamic_slice_in_dim(
        mr_filter, chan_offset // GROUP, max(1, narrow // GROUP), axis=0
    )
    skip_here = lax.dynamic_slice_in_dim(mr_skip, chan_offset, narrow)
    gain_here = lax.dynamic_slice_in_dim(norm_gain, chan_offset, narrow)
    zero_rows = jnp.zeros((narrow, MR), jnp.bfloat16)
    mixed_rows = long_conv(
        product_rows, zero_rows, group_rows.astype(jnp.bfloat16), starts
    ) + skip_here[:, None] * product_rows.astype(jnp.float32)
    gated = gate_conv * mixed_rows
    shares = lax.psum_scatter(
        jnp.sum(gated * gated, axis=0).astype(jnp.bfloat16), "ctx", scatter_dimension=0, tiled=True
    ).astype(jnp.float32)
    own_scale = lax.rsqrt(row_total(shares) / D + NORM_EPS)
    row_scale = lax.all_gather(own_scale, "ctx", axis=0, tiled=True)
    return (gated * row_scale[None, :] * gain_here[:, None]).astype(jnp.bfloat16)


def solution(mesh):
    in_specs = (
        P("ch", "ctx"),
        P("ch", "ctx"),
        P("ch", "ctx"),
        P(None, None, "ch"),
        P("ch", None),
        P("ch"),
        P("ch"),
        P(),
    )
    out_specs = P(("ch", "ctx"), None)
    return jax.shard_map(local, mesh=mesh, in_specs=in_specs, out_specs=out_specs, check_vma=False)
```

profile of v0, /device:TPU:1, one launch (start us, length us, event | category | flops | bytes accessed | tf_op | source)
XLA Modules:
  0.0 279.0 jit_solution(16619326890867095155)
XLA Ops:
  0.0 0.0 copy-start
  0.0 2.2 pad_maximum_fusion
  2.2 4.7 %copy.30 = bf16[3,1024,512]{2,0,1:T(4,128)(2,1)} copy(bf16[3,1024,512]{2,1,0:T(8,128)(2,1)S(1)} %pad_maximum_fusion) | data formatting | bytes 6291456 | tf_op jit(solution)/shard_map/stack | solution.py:99
  6.9 0.0 copy-start.2
  6.9 8.8 %all-to-all-start = ((bf16[3,1024,512]{2,0,1:T(4,128)(2,1)}), bf16[3,1024,512]{2,0,1:T(4,128)(2,1)}, u32[]{:S(2)}, u32[]{:S(2)}) async-start(bf16[3,1024,512]{2,0,1:T(4,128)(2,1)} %copy.30), calls=%async_computation | async-start | bytes 8388608 | tf_op jit(solution)/shard_map/all_to_all | solution.py:100
  15.7 0.0 copy-start.3
  15.7 0.0 copy-done.2
  15.7 0.1 copy.29
  15.8 0.1 reduce-window.9
  15.9 0.1 reduce
  16.1 0.0 copy-done
  16.2 1.3 tile.10
  17.5 0.3 slice.128
  17.9 0.8 dynamic_slice.34
  18.7 0.8 dynamic_slice.35
  19.4 0.0 copy-done.3
  19.4 0.6 dynamic-slice
  20.6 0.9 fusion.34
  21.5 0.8 select_reduce_fusion
  22.3 45.5 %all-to-all-done = bf16[3,1024,512]{2,0,1:T(4,128)(2,1)} async-done(((bf16[3,1024,512]{2,0,1:T(4,128)(2,1)}), bf16[3,1024,512]{2,0,1:T(4,128)(2,1)}, u32[]{:S(2)}, u32[]{:S(2)}) %all-to-all-start) | async-done | bytes 3145760 | tf_op jit(solution)/shard_map/all_to_all | solution.py:100
  67.9 11.2 %fusion.39 = (bf16[1,32,32,512]{3,0,1,2:T(2,128)(2,1)}, bf16[1,32,32,512]{3,0,1,2:T(2,128)(2,1)S(1)}, bf16[1,32,32,512]{3,0,1,2:T(2,128)(2,1)S(1)}) fusion(bf16[3,32,32,512]{3,0,1,2:T(4,128)(2,1)} %bitcast.6), kind=kLoop, calls=%fused_computation.77 | loop fusion | bytes 6291456 | tf_op jit(solution)/shard_map/slice | solution.py:109
  79.0 1.1 copy.33
  80.1 0.6 copy.43
  80.7 1.1 copy.32
  81.9 0.6 copy.42
  82.4 0.7 pad_convert_fusion
  83.2 2.4 fusion.18
  85.6 0.1 concatenate.22
  85.7 0.5 reshape.144
  86.2 0.6 fusion.40
  86.8 0.3 pad_maximum_fusion.1
  87.1 1.6 broadcast_in_dim.159.clone
  88.7 15.0 %while.16 = (s32[]{:T(128)}, f32[2,16,128,128]{3,2,1,0:T(8,128)}, s32[128,128]{1,0:T(8,128)S(1)}, bf16[2,256,128]{2,1,0:T(8,128)(2,1)S(1)}, bf16[2,16,128,256]{3...) while((s32[]{:T(128)}, f32[2,16,128,128]{3,2,1,0:T(8,128)}, ...), condition=%wide.region_3.4_spmd.clone, body=%wide.region_2.3_spmd.clone.sunk | while | flops 70263112 | bytes 5491127 | solution.py:82
  88.7 0.1 broadcast_add_fusion.2
  88.8 1.4 broadcast_compare_fusion.2
  90.3 1.2 fusion.46
  91.5 1.0 copy_dynamic-update-slice_fusion.2
  92.5 0.1 broadcast_add_fusion.2
  92.5 1.4 broadcast_compare_fusion.2
  94.0 1.2 fusion.46
  95.2 1.0 copy_dynamic-update-slice_fusion.2
  96.2 0.1 broadcast_add_fusion.2
  96.3 1.4 broadcast_compare_fusion.2
  97.7 1.2 fusion.46
  98.9 1.0 copy_dynamic-update-slice_fusion.2
  100.0 0.1 broadcast_add_fusion.2
  100.0 1.4 broadcast_compare_fusion.2
  101.5 1.2 fusion.46
  102.7 1.0 copy_dynamic-update-slice_fusion.2
  103.7 2.7 copy.31
  106.4 0.6 copy.40
  107.0 0.0 copy-start.1
  107.0 0.3 pad_convert_fusion.2
  107.4 1.2 copy-done.1
  108.6 2.3 multiply_reduce_fusion
  110.9 120.1 %all-reduce.4 = bf16[16384]{0:T(1024)(128)(2,1)S(1)} all-reduce(bf16[16384]{0:T(1024)(128)(2,1)S(1)} %get-tuple-element.225), channel_id=2, replica_groups=mesh['ctx'=32,'ch'=8] {'ctx'}, use_global_device_ids=true, to_apply=%region_5.6.clone | all-reduce | flops 16384 | bytes 65536
  231.0 0.1 dynamic-slice_convert_fusion
  231.1 16.5 %psum.7 = f32[512]{0:T(512)S(1)} all-reduce(f32[512]{0:T(512)S(1)} %dynamic-slice_convert_fusion), channel_id=1, replica_groups=mesh['ctx'=32,'ch'=8] {'ch'}, use_global_device_ids=true, to_apply=%region_6.7 | all-reduce | flops 512 | bytes 4096 | tf_op jit(solution)/shard_map/psum | solution.py:92
  247.6 30.2 %all-gather = f32[32,1,512]{2,1,0:T(1,128)S(1)} all-gather(f32[1,1,512]{2,1,0:T(1,128)S(1)} %bitcast.69), channel_id=1, replica_groups=mesh['ctx'=32,'ch'=8] {'ctx'}, dimensions={0}, use_global_device_ids=true | all-gather | bytes 67584 | tf_op jit(solution)/shard_map/all_gather | solution.py:129
  277.8 1.2 multiply_convert_fusion
  (28 shorter events, 0.4 us)
Async XLA Ops:
  0.0 16.1 %copy-start = (f32[64,128]{1,0:T(8,128)S(1)}, f32[64,128]{1,0:T(8,128)}, u32[]{:S(2)}) copy-start(f32[64,128]{1,0:T(8,128)} %param.14) | copy-start | bytes 98308
  6.9 8.8 %copy-start.2 = (s32[64]{0:T(128)S(1)}, s32[64]{0:T(128)}, u32[]{:S(2)}) copy-start(s32[64]{0:T(128)} %param.17) | copy-start | bytes 772
  6.9 61.0 %all-to-all-start = ((bf16[3,1024,512]{2,0,1:T(4,128)(2,1)}), bf16[3,1024,512]{2,0,1:T(4,128)(2,1)}, u32[]{:S(2)}, u32[]{:S(2)}) async-start(bf16[3,1024,512]{2,0,1:T(4,128)(2,1)} %copy.30), calls=%async_computation | async-start | bytes 8388608 | tf_op jit(solution)/shard_map/all_to_all | solution.py:100
  15.7 3.7 %copy-start.3 = (u32[256]{0:T(256)S(1)}, u32[256]{0:T(256)}, u32[]{:S(2)}) copy-start(u32[256]{0:T(256)} %constant.121) | copy-start | bytes 3076
  107.0 1.6 copy-start.1
where the time goes:
time: 279 us
  blocking collectives  167 us (60%)
  waiting for transfers between devices  45.5 us (16%)
  local copies, waits for them, and re-layouts  35.5 us (13%)
  other arithmetic  16.6 us (6%)
  starting transfers between devices  8.79 us (3%)
  matrix products  4.89 us (2%)
    unnamed x1, blocking collectives  120 us
    all_to_all x1, waiting for transfers between devices, local(): lax.all_to_all(stacked, 'ctx', split_axis=1, concat_axis=2, tiled=True)  45.5 us
    all_gather x1, blocking collectives, local(): row_scale = lax.all_gather(own_scale, 'ctx', axis=0, tiled=True)  30.2 us
    psum x1, blocking collectives, row_total(): return lax.psum(partial_value, 'ch')  16.5 us
    slice x2, local copies, waits for them, and re-layouts, local(): received[0]  13.9 us
    all_to_all x1, starting transfers between devices, local(): lax.all_to_all(stacked, 'ctx', split_axis=1, concat_axis=2, tiled=True)  8.79 us
  transfers between devices with their start and end apart: 1, of which 1 were waited for; matrix products, arithmetic and copies ran while one was open for 2% of the time, Pallas kernels for 0%

commit v1 on v0

--- a/solution.py
+++ b/solution.py
@@ -126,7 +126,10 @@
         jnp.sum(gated * gated, axis=0).astype(jnp.bfloat16), "ctx", scatter_dimension=0, tiled=True
     ).astype(jnp.float32)
     own_scale = lax.rsqrt(row_total(shares) / D + NORM_EPS)
-    row_scale = lax.all_gather(own_scale, "ctx", axis=0, tiled=True)
+    far_arr = lax.axis_size("ctx")
+    row_scale = jnp.concatenate(
+        lax.all_to_all(jnp.stack(far_arr * [own_scale], axis=0), "ctx", 0, 0), axis=0
+    )
     return (gated * row_scale[None, :] * gain_here[:, None]).astype(jnp.bfloat16)
 
 

time: 279 us -> 270 us (0.968)
  blocking collectives: 167 us -> 137 us
  starting transfers between devices: 8.79 us -> 21.5 us
  waiting for transfers between devices: 45.5 us -> 53 us
    all_gather x1 -> x0, blocking collectives: 30.2 us -> none  [local(): row_scale = lax.all_gather(own_scale, 'ctx', axis=0, tiled=True)]
    all_to_all x0 -> x1, starting transfers between devices: none -> 12.7 us  [local(): lax.all_to_all(jnp.stack(far_arr * [own_scale], axis=0), 'ctx', 0, 0)]
    all_to_all x0 -> x1, waiting for transfers between devices: none -> 6.71 us  [local(): lax.all_to_all(jnp.stack(far_arr * [own_scale], axis=0), 'ctx', 0, 0)]
  transfers between devices with their start and end apart: 1 -> 2, of which waited for: 1 -> 2; matrix products, arithmetic and copies ran while one was open for 2% -> 2% of each run, Pallas kernels for 0% -> 0%
where the time goes in v1:
time: 270 us
  blocking collectives  137 us (51%)
  waiting for transfers between devices  53 us (20%)
  local copies, waits for them, and re-layouts  36.2 us (13%)
  starting transfers between devices  21.5 us (8%)
  other arithmetic  16.6 us (6%)
  matrix products  4.89 us (2%)
    unnamed x1, blocking collectives  120 us
    all_to_all x1, waiting for transfers between devices, local(): lax.all_to_all(stacked, 'ctx', split_axis=1, concat_axis=2, tiled=True)  46.3 us
    psum x1, blocking collectives, row_total(): return lax.psum(partial_value, 'ch')  16.5 us
    slice x2, local copies, waits for them, and re-layouts, local(): received[0]  13.9 us
    all_to_all x1, starting transfers between devices, local(): lax.all_to_all(jnp.stack(far_arr * [own_scale], axis=0), 'ctx', 0, 0)  12.7 us
    all_to_all x1, starting transfers between devices, local(): lax.all_to_all(stacked, 'ctx', split_axis=1, concat_axis=2, tiled=True)  8.79 us
    all_to_all x1, waiting for transfers between devices, local(): lax.all_to_all(jnp.stack(far_arr * [own_scale], axis=0), 'ctx', 0, 0)  6.71 us
    ge x4, other arithmetic, advance(): allowed = sources[:, :, None] >= row_starts[:, None, :]  5.57 us
  transfers between devices with their start and end apart: 2, of which 2 were waited for; matrix products, arithmetic and copies ran while one was open for 2% of the time, Pallas kernels for 0%

profile of v1, /device:TPU:1, one launch (start us, length us, event | category | flops | bytes accessed | tf_op | source)
XLA Modules:
  0.0 269.6 jit_solution(4944869704943773677)
XLA Ops:
  0.0 0.0 copy-start
  0.0 2.2 pad_maximum_fusion
  2.2 4.7 %copy.30 = bf16[3,1024,512]{2,0,1:T(4,128)(2,1)} copy(bf16[3,1024,512]{2,1,0:T(8,128)(2,1)S(1)} %pad_maximum_fusion) | data formatting | bytes 6291456 | tf_op jit(solution)/shard_map/stack | solution.py:99
  6.9 0.0 copy-start.2
  6.9 8.8 %all-to-all-start = ((bf16[3,1024,512]{2,0,1:T(4,128)(2,1)}), bf16[3,1024,512]{2,0,1:T(4,128)(2,1)}, u32[]{:S(2)}, u32[]{:S(2)}) async-start(bf16[3,1024,512]{2,0,1:T(4,128)(2,1)} %copy.30), calls=%async_computation | async-start | bytes 8388608 | tf_op jit(solution)/shard_map/all_to_all | solution.py:100
  15.7 0.0 copy-start.3
  15.7 0.0 copy-done.2
  15.7 0.1 copy.29
  15.8 0.1 reduce-window.9
  15.9 0.1 reduce
  16.1 0.0 copy-done
  16.2 1.3 tile.10
  17.5 0.3 slice.128
  17.9 0.8 dynamic_slice.34
  18.7 0.0 copy-done.3
  18.7 0.6 dynamic-slice
  19.8 0.9 fusion.34
  20.7 0.8 select_reduce_fusion
  21.6 46.3 %all-to-all-done = bf16[3,1024,512]{2,0,1:T(4,128)(2,1)} async-done(((bf16[3,1024,512]{2,0,1:T(4,128)(2,1)}), bf16[3,1024,512]{2,0,1:T(4,128)(2,1)}, u32[]{:S(2)}, u32[]{:S(2)}) %all-to-all-start) | async-done | bytes 3145760 | tf_op jit(solution)/shard_map/all_to_all | solution.py:100
  67.9 11.2 %fusion.39 = (bf16[1,32,32,512]{3,0,1,2:T(2,128)(2,1)}, bf16[1,32,32,512]{3,0,1,2:T(2,128)(2,1)S(1)}, bf16[1,32,32,512]{3,0,1,2:T(2,128)(2,1)S(1)}) fusion(bf16[3,32,32,512]{3,0,1,2:T(4,128)(2,1)} %bitcast.6), kind=kLoop, calls=%fused_computation.77 | loop fusion | bytes 6291456 | tf_op jit(solution)/shard_map/slice | solution.py:109
  79.0 1.1 copy.33
  80.1 0.6 copy.43
  80.7 1.1 copy.32
  81.9 0.6 copy.42
  82.4 0.7 pad_convert_fusion
  83.2 2.4 fusion.18
  85.6 0.1 concatenate.22
  85.7 0.5 reshape.152
  86.2 0.6 fusion.40
  86.8 0.3 pad_maximum_fusion.1
  87.1 1.6 broadcast_in_dim.158.clone
  88.7 15.0 %while.16 = (s32[]{:T(128)}, f32[2,16,128,128]{3,2,1,0:T(8,128)}, s32[128,128]{1,0:T(8,128)S(1)}, bf16[2,256,128]{2,1,0:T(8,128)(2,1)S(1)}, bf16[2,16,128,256]{3...) while((s32[]{:T(128)}, f32[2,16,128,128]{3,2,1,0:T(8,128)}, ...), condition=%wide.region_3.4_spmd.clone, body=%wide.region_2.3_spmd.clone.sunk | while | flops 70263112 | bytes 5491127 | solution.py:82
  88.7 0.1 broadcast_add_fusion.2
  88.8 1.4 broadcast_compare_fusion.2
  90.3 1.2 fusion.46
  91.5 1.0 copy_dynamic-update-slice_fusion.2
  92.5 0.1 broadcast_add_fusion.2
  92.5 1.4 broadcast_compare_fusion.2
  94.0 1.2 fusion.46
  95.2 1.0 copy_dynamic-update-slice_fusion.2
  96.2 0.1 broadcast_add_fusion.2
  96.3 1.4 broadcast_compare_fusion.2
  97.7 1.2 fusion.46
  98.9 1.0 copy_dynamic-update-slice_fusion.2
  100.0 0.1 broadcast_add_fusion.2
  100.0 1.4 broadcast_compare_fusion.2
  101.5 1.2 fusion.46
  102.7 1.0 copy_dynamic-update-slice_fusion.2
  103.7 2.7 %copy.31 = bf16[1,32,32,512]{3,2,1,0:T(8,128)(2,1)S(1)} copy(bf16[1,32,32,512]{3,0,1,2:T(2,128)(2,1)} %get-tuple-element.227) | data formatting | bytes 2097152 | tf_op jit(solution)/shard_map/slice | solution.py:109
  106.4 0.6 copy.40
  107.0 0.0 copy-start.1
  107.0 0.3 pad_convert_fusion.2
  107.4 1.2 copy-done.1
  108.6 2.3 multiply_reduce_fusion
  110.9 120.1 %all-reduce.4 = bf16[16384]{0:T(1024)(128)(2,1)S(1)} all-reduce(bf16[16384]{0:T(1024)(128)(2,1)S(1)} %get-tuple-element.225), channel_id=2, replica_groups=mesh['ctx'=32,'ch'=8] {'ctx'}, use_global_device_ids=true, to_apply=%region_5.6.clone | all-reduce | flops 16384 | bytes 65536
  231.0 0.1 dynamic-slice_convert_fusion
  231.1 16.5 %psum.7 = f32[512]{0:T(512)S(1)} all-reduce(f32[512]{0:T(512)S(1)} %dynamic-slice_convert_fusion), channel_id=1, replica_groups=mesh['ctx'=32,'ch'=8] {'ch'}, use_global_device_ids=true, to_apply=%region_6.7 | all-reduce | flops 512 | bytes 4096 | tf_op jit(solution)/shard_map/psum | solution.py:92
  247.6 0.7 stack.14
  248.3 12.7 %all-to-all-start.1 = ((f32[32,1,512]{2,1,0:T(1,128)}), f32[32,1,512]{2,1,0:T(1,128)S(1)}, u32[]{:S(2)}, u32[]{:S(2)}) async-start(f32[32,1,512]{2,1,0:T(1,128)} %stack.14), calls=%async_computation.1 | async-start | bytes 131072 | tf_op jit(solution)/shard_map/all_to_all | solution.py:131
  260.9 0.8 dynamic_slice.35
  261.7 6.7 %all-to-all-done.1 = f32[32,1,512]{2,1,0:T(1,128)S(1)} async-done(((f32[32,1,512]{2,1,0:T(1,128)}), f32[32,1,512]{2,1,0:T(1,128)S(1)}, u32[]{:S(2)}, u32[]{:S(2)}) %all-to-all-start.1) | async-done | bytes 65568 | tf_op jit(solution)/shard_map/all_to_all | solution.py:131
  268.4 1.2 multiply_convert_fusion
  (28 shorter events, 0.4 us)
Async XLA Ops:
  0.0 16.1 %copy-start = (f32[64,128]{1,0:T(8,128)S(1)}, f32[64,128]{1,0:T(8,128)}, u32[]{:S(2)}) copy-start(f32[64,128]{1,0:T(8,128)} %param.14) | copy-start | bytes 98308
  6.9 8.8 %copy-start.2 = (s32[64]{0:T(128)S(1)}, s32[64]{0:T(128)}, u32[]{:S(2)}) copy-start(s32[64]{0:T(128)} %param.17) | copy-start | bytes 772
  6.9 61.0 %all-to-all-start = ((bf16[3,1024,512]{2,0,1:T(4,128)(2,1)}), bf16[3,1024,512]{2,0,1:T(4,128)(2,1)}, u32[]{:S(2)}, u32[]{:S(2)}) async-start(bf16[3,1024,512]{2,0,1:T(4,128)(2,1)} %copy.30), calls=%async_computation | async-start | bytes 8388608 | tf_op jit(solution)/shard_map/all_to_all | solution.py:100
  15.7 3.0 %copy-start.3 = (u32[256]{0:T(256)S(1)}, u32[256]{0:T(256)}, u32[]{:S(2)}) copy-start(u32[256]{0:T(256)} %constant.121) | copy-start | bytes 3076
  107.0 1.6 copy-start.1
  248.3 20.2 %all-to-all-start.1 = ((f32[32,1,512]{2,1,0:T(1,128)}), f32[32,1,512]{2,1,0:T(1,128)S(1)}, u32[]{:S(2)}, u32[]{:S(2)}) async-start(f32[32,1,512]{2,1,0:T(1,128)} %stack.14), calls=%async_computation.1 | async-start | bytes 131072 | tf_op jit(solution)/shard_map/all_to_all | solution.py:131
